TPU v7x, 32 devices: a whole 2x2x4 slice. The times are simulated.
32 devices in a mesh: gz: 8 (over z, x), gy: 4 (over y, core).
Axes of the slice: x: 2, y: 2, z: 4, core: 2. Of those that a mesh axis runs over, the one named last changes fastest.
Arguments:
- volume: bfloat16 [32, 16, 32, 128], P('gz', 'gy'), may hold values from -6 to 6
- kernel_a: bfloat16 [3, 3, 3, 128, 128], replicated, may hold values from -0.109375 to 0.109375
- bias_a: float32 [128], replicated, may hold values from -3 to 3
- kernel_b: bfloat16 [3, 3, 3, 128, 256], P(None, None, None, None, 'gy'), may hold values from -0.109375 to 0.109375
- bias_b: float32 [256], P('gy'), may hold values from -3 to 3
- kernel_c: bfloat16 [3, 3, 3, 256, 512], P(None, None, None, None, 'gy'), may hold values from -0.078125 to 0.078125
- bias_c: float32 [512], P('gy'), may hold values from -3 to 3
Outputs:
- skip_a: bfloat16 [32, 16, 32, 128], P('gz', 'gy')
- skip_b: bfloat16 [16, 8, 16, 256], P('gz', None, None, 'gy')
- bottom: bfloat16 [8, 4, 8, 512], P('gz', None, None, 'gy')
All inputs are finite; a program needn't handle non-finite values.
Results may differ from a plain program's by a relative error of at most 0.0054.
Values may be sent and summed in bfloat16 or wider, within the bound.
A program may use at most 64 MiB of HBM per device.

v0:
```python
import jax
import jax.numpy as jnp
from jax import lax
from jax.sharding import PartitionSpec as P


def extended(array, sides, width):
    for axis, dim in sides:
        peers, length = (lax.axis_size(axis), array.shape[dim])
        up = [(i, (i + 1) % peers) for i in range(peers - 1)]
        down = [(j, i) for i, j in up]
        last = lax.slice_in_dim(array, length - width, length, axis=dim)
        first = lax.slice_in_dim(array, 0, width, axis=dim)
        before = lax.ppermute(last, axis, up)
        after = lax.ppermute(first, axis, down)
        array = jnp.concatenate([before, array, after], axis=dim)
    return array


def conv_relu(padded, kernel, bias):
    out = lax.conv_general_dilated(
        padded[None],
        kernel,
        (1, 1, 1),
        ((0, 0), (0, 0), (1, 1)),
        dimension_numbers=("NDHWC", "DHWIO", "NDHWC"),
        preferred_element_type=jnp.float32,
    )[0]
    return jnp.maximum(out + bias, 0.0).astype(jnp.bfloat16)


def shrink(field):
    depth, height, width, chans = field.shape
    blocks = field.reshape(depth // 2, 2, height // 2, 2, width // 2, 2, chans)
    return jnp.max(blocks, axis=(1, 3, 5))


def pad_height(field):
    return jnp.pad(field, ((0, 0), (1, 1), (0, 0), (0, 0)))


def on_device(volume, kernel_a, bias_a, kernel_b, bias_b, kernel_c, bias_c):
    padded = extended(volume, (("gz", 0), ("gy", 1)), 1)
    skip_a = conv_relu(padded, kernel_a, bias_a)
    pooled_a = shrink(skip_a)
    gathered = lax.all_gather(pooled_a, "gy", axis=1, tiled=True)
    ready_b = extended(gathered, (("gz", 0),), 1)
    skip_b = conv_relu(pad_height(ready_b), kernel_b, bias_b)
    pooled_b = shrink(skip_b)
    widened = lax.all_gather(pooled_b, "gy", axis=3, tiled=True)
    ready_c = extended(widened, (("gz", 0),), 1)
    bottom = conv_relu(pad_height(ready_c), kernel_c, bias_c)
    return (skip_a, skip_b, bottom)


def solution(mesh):
    return jax.shard_map(
        on_device,
        mesh=mesh,
        in_specs=(
            P("gz", "gy", None, None),
            P(),
            P(),
            P(None, None, None, None, "gy"),
            P("gy"),
            P(None, None, None, None, "gy"),
            P("gy"),
        ),
        out_specs=(P("gz", "gy", None, None), P("gz", None, None, "gy"), P("gz", None, None, "gy")),
        check_vma=False,
    )
```

profile of v0, /device:TPU:24, one launch (start us, length us, event | category | flops | bytes accessed | tf_op | source)
XLA Modules:
  0.0 54.5 jit_solution(7939145247504538104)
XLA Ops:
  0.6 0.0 copy-start
  0.6 0.9 %fusion.45 = (bf16[1,4,32,128]{3,2,1,0:T(8,128)(2,1)S(1)}, bf16[1,4,32,128]{3,2,1,0:T(8,128)(2,1)S(1)}) fusion(bf16[4,4,32,128]{3,2,1,0:T(8,128)(2,1)} %param.7), kind=kLoop, calls=%fused_computation.61 | loop fusion | bytes 131072 | tf_op jit(solution)/shard_map/slice | solution.py:13
  1.6 3.4 %collective-permute-start = (bf16[1,4,32,128]{3,2,1,0:T(8,128)(2,1)S(1)}, bf16[1,4,32,128]{3,2,1,0:T(8,128)(2,1)S(1)}, u32[]{:S(2)}, u32[]{:S(2)}) collective-permute-start(bf16[1,4,32,128]{3,2,1,0:T(8,128)(2,1)S(1)} %get-tuple-element.15), channel_id=1, source_target_pairs={{0,4},{4,8},{8,12},{12,16},{16,20},{20,24},{24,28},{1,5},{5,9},{9,... | collective-permute-start | bytes 98312 | tf_op jit(solution)/shard_map/ppermute | solution.py:14
  5.0 3.3 %collective-permute-start.1 = (bf16[1,4,32,128]{3,2,1,0:T(8,128)(2,1)S(1)}, bf16[1,4,32,128]{3,2,1,0:T(8,128)(2,1)S(1)}, u32[]{:S(2)}, u32[]{:S(2)}) collective-permute-start(bf16[1,4,32,128]{3,2,1,0:T(8,128)(2,1)S(1)} %get-tuple-element.14), channel_id=1, source_target_pairs={{4,0},{8,4},{12,8},{16,12},{20,16},{24,20},{28,24},{5,1},{9,5},{13... | collective-permute-start | bytes 98312 | tf_op jit(solution)/shard_map/ppermute | solution.py:15
  8.3 0.0 collective-permute-done
  8.3 0.9 %constant_dynamic-update-slice_fusion.1 = bf16[6,4,32,128]{3,2,1,0:T(8,128)(2,1)S(1)} fusion(bf16[6,4,32,128]{3,2,1,0:T(8,128)(2,1)S(1)} %constant_dynamic-update-slice_fusion.2, bf16[4,4,32,128]{3,2,1,0:T(8,128)(2,1)} %param.7), kind=kLoop, calls=%fused_computation.52 | loop fusion | bytes 262144
  9.3 1.5 %collective-permute-done.1 = bf16[1,4,32,128]{3,2,1,0:T(8,128)(2,1)S(1)} collective-permute-done((bf16[1,4,32,128]{3,2,1,0:T(8,128)(2,1)S(1)}, bf16[1,4,32,128]{3,2,1,0:T(8,128)(2,1)S(1)}, u32[]{:S(2)}, u32[]{:S(2)}) %collective-permute-start.1) | collective-permute-done | bytes 32800 | tf_op jit(solution)/shard_map/ppermute | solution.py:15
  10.8 0.0 copy-start.6
  10.8 1.4 %collective-permute-start.2 = (bf16[6,1,32,128]{3,2,1,0:T(8,128)(2,1)S(1)}, bf16[6,1,32,128]{3,2,1,0:T(8,128)(2,1)S(1)}, u32[]{:S(2)}, u32[]{:S(2)}) collective-permute-start(bf16[6,1,32,128]{3,2,1,0:T(8,128)(2,1)S(1)} %get-tuple-element.12), channel_id=1, source_target_pairs={{0,1},{1,2},{2,3},{4,5},{5,6},{6,7},{8,9},{9,10},{10,11},{12,13},{... | collective-permute-start | bytes 147464 | tf_op jit(solution)/shard_map/ppermute | solution.py:14
  12.2 1.3 %collective-permute-start.3 = (bf16[6,1,32,128]{3,2,1,0:T(8,128)(2,1)S(1)}, bf16[6,1,32,128]{3,2,1,0:T(8,128)(2,1)S(1)}, u32[]{:S(2)}, u32[]{:S(2)}) collective-permute-start(bf16[6,1,32,128]{3,2,1,0:T(8,128)(2,1)S(1)} %get-tuple-element.13), channel_id=1, source_target_pairs={{1,0},{2,1},{3,2},{5,4},{6,5},{7,6},{9,8},{10,9},{11,10},{13,12},{... | collective-permute-start | bytes 147464 | tf_op jit(solution)/shard_map/ppermute | solution.py:15
  13.5 0.0 collective-permute-done.2
  13.5 3.6 %collective-permute-done.3 = bf16[6,1,32,128]{3,2,1,0:T(8,128)(2,1)S(1)} collective-permute-done((bf16[6,1,32,128]{3,2,1,0:T(8,128)(2,1)S(1)}, bf16[6,1,32,128]{3,2,1,0:T(8,128)(2,1)S(1)}, u32[]{:S(2)}, u32[]{:S(2)}) %collective-permute-start.3) | collective-permute-done | bytes 49184 | tf_op jit(solution)/shard_map/ppermute | solution.py:15
  17.2 0.1 copy.50
  17.3 0.1 pad.10.clone
  17.4 0.1 copy.37
  17.5 0.0 copy-done.4
  17.5 0.0 copy-done.6
  17.5 0.0 copy-start.1
  17.5 1.3 %convolution_select_fusion = f32[4,4,8,5,128]{4,2,3,1,0:T(8,128)S(1)} fusion(bf16[3,3,3,128,128]{4,3,2,1,0:T(8,128)(2,1)S(1)} %copy-done.4, bf16[6,6,1,7,2,128]{5,3,4,1,0,2:T(8,128)(2,1)S(1)} %slice.31, bf16[6,6,1,8,5,128]{5,3,4,1,0,2:T(8,128)(2,1)S(1)} %copy.37, pred[8,5]{0,1:T(8,128)(4,1)S(1)} %copy-done.6), kind=kOutput, calls=%fused_computation | convolution fusion | flops 567861248 | bytes 1710120 | tf_op jit(solution)/shard_map/conv_general_dilated | solution.py:21
  18.9 0.1 copy.38
  18.9 0.0 copy-start.2
  19.0 0.0 copy-start.5
  19.0 0.0 copy-start.7
  19.0 0.0 copy-done.1
  19.0 0.2 fusion.31
  19.2 6.7 %all_gather.6 = bf16[2,8,16,128]{3,2,0,1:T(8,128)(2,1)S(1)} all-gather(bf16[2,2,16,128]{3,2,0,1:T(8,128)(2,1)S(1)} %copy.39), channel_id=1, replica_groups=mesh['gz'=8,'gy'=4] {'gy'}, dimensions={1}, use_global_device_ids=true | all-gather | bytes 81920 | tf_op jit(solution)/shard_map/all_gather | solution.py:46
  25.9 1.9 %collective-permute-start.4 = (bf16[1,8,16,128]{3,2,0,1:T(8,128)(2,1)S(1)}, bf16[1,8,16,128]{3,2,0,1:T(8,128)(2,1)S(1)}, u32[]{:S(2)}, u32[]{:S(2)}) collective-permute-start(bf16[1,8,16,128]{3,2,0,1:T(8,128)(2,1)S(1)} %get-tuple-element.16), channel_id=1, source_target_pairs={{0,4},{4,8},{8,12},{12,16},{16,20},{20,24},{24,28},{1,5},{5,9},{9,... | collective-permute-start | bytes 98312 | tf_op jit(solution)/shard_map/ppermute | solution.py:14
  27.9 4.8 %collective-permute-start.5 = (bf16[1,8,16,128]{3,2,0,1:T(8,128)(2,1)S(1)}, bf16[1,8,16,128]{3,2,0,1:T(8,128)(2,1)S(1)}, u32[]{:S(2)}, u32[]{:S(2)}) collective-permute-start(bf16[1,8,16,128]{3,2,0,1:T(8,128)(2,1)S(1)} %get-tuple-element.17), channel_id=1, source_target_pairs={{4,0},{8,4},{12,8},{16,12},{20,16},{24,20},{28,24},{5,1},{9,5},{13... | collective-permute-start | bytes 98312 | tf_op jit(solution)/shard_map/ppermute | solution.py:15
  32.7 0.1 fusion.16
  32.8 0.7 %copy.48 = bf16[4,4,32,128]{3,2,1,0:T(8,128)(2,1)} copy(bf16[4,4,32,128]{3,1,2,0:T(4,128)(2,1)S(1)} %fusion.16) | data formatting | bytes 262144
  33.4 0.0 collective-permute-done.4
  33.4 0.8 %collective-permute-done.5 = bf16[1,8,16,128]{3,2,0,1:T(8,128)(2,1)S(1)} collective-permute-done((bf16[1,8,16,128]{3,2,0,1:T(8,128)(2,1)S(1)}, bf16[1,8,16,128]{3,2,0,1:T(8,128)(2,1)S(1)}, u32[]{:S(2)}, u32[]{:S(2)}) %collective-permute-start.5) | collective-permute-done | bytes 32800 | tf_op jit(solution)/shard_map/ppermute | solution.py:15
  34.3 0.1 copy.51
  34.4 0.1 pad.12.clone
  34.5 0.0 copy-done.2
  34.6 0.8 %maximum_convert_fusion.1 = (bf16[2,8,8,3,64]{4,2,3,1,0:T(8,128)(2,1)S(1)}, f32[2,8,8,3,64]{4,2,3,1,0:T(8,128)S(1)}) fusion(f32[64]{0:T(128)S(1)} %copy-done.2, bf16[3,3,3,128,64]{3,4,2,1,0:T(8,128)(2,1)S(1)} %copy-done.5, bf16[4,10,1,7,2,128]{5,3,4,1,0,2:T(8,128)(2,1)S(1)} %slice.35, bf16[4,10,1,8,3,128]{5,3,4,1,0,2:T(8,128)(2,1)S(1)} %copy.42, ...), kind=kOutput, calls=%fused_computation.28 | convolution fusion | flops 171196416 | bytes 979224 | tf_op jit(solution)/shard_map/conv_general_dilated | solution.py:21
  35.5 0.1 reduce_max.30
  35.5 0.1 copy.45
  35.7 5.8 %all-gather = bf16[4,8,256]{1,0,2:T(4,128)(2,1)S(1)} all-gather(bf16[4,8,64]{1,0,2:T(4,128)(2,1)S(1)} %copy.45), channel_id=2, replica_groups=mesh['gz'=8,'gy'=4] {'gy'}, dimensions={2}, use_global_device_ids=true | all-gather | bytes 20480 | tf_op jit(solution)/shard_map/all_gather | solution.py:50
  41.5 0.1 copy.46
  41.6 5.1 %collective-permute-start.7 = (bf16[1,4,8,256]{3,2,1,0:T(8,128)(2,1)S(1)}, bf16[1,4,8,256]{3,2,1,0:T(8,128)(2,1)S(1)}, u32[]{:S(2)}, u32[]{:S(2)}) collective-permute-start(bf16[1,4,8,256]{3,2,1,0:T(8,128)(2,1)S(1)} %bitcast.48), channel_id=1, source_target_pairs={{4,0},{8,4},{12,8},{16,12},{20,16},{24,20},{28,24},{5,1},{9,5},{13... | collective-permute-start | bytes 49160 | tf_op jit(solution)/shard_map/ppermute | solution.py:15
  46.7 1.9 %collective-permute-start.6 = (bf16[1,4,8,256]{3,2,1,0:T(8,128)(2,1)S(1)}, bf16[1,4,8,256]{3,2,1,0:T(8,128)(2,1)S(1)}, u32[]{:S(2)}, u32[]{:S(2)}) collective-permute-start(bf16[1,4,8,256]{3,2,1,0:T(8,128)(2,1)S(1)} %bitcast.49), channel_id=1, source_target_pairs={{0,4},{4,8},{8,12},{12,16},{16,20},{20,24},{24,28},{1,5},{5,9},{9,... | collective-permute-start | bytes 49160 | tf_op jit(solution)/shard_map/ppermute | solution.py:14
  48.7 0.0 copy-start.3
  48.8 0.6 %copy.49 = bf16[2,8,16,64]{3,2,1,0:T(8,128)(2,1)} copy(bf16[2,8,16,64]{3,1,2,0:T(8,128)(2,1)S(1)} %fusion.30) | data formatting | bytes 65536
  49.4 0.0 collective-permute-done.7
  49.4 3.9 %collective-permute-done.6 = bf16[1,4,8,256]{3,2,1,0:T(8,128)(2,1)S(1)} collective-permute-done((bf16[1,4,8,256]{3,2,1,0:T(8,128)(2,1)S(1)}, bf16[1,4,8,256]{3,2,1,0:T(8,128)(2,1)S(1)}, u32[]{:S(2)}, u32[]{:S(2)}) %collective-permute-start.6) | collective-permute-done | bytes 16416 | tf_op jit(solution)/shard_map/ppermute | solution.py:14
  53.3 0.6 %fusion.25 = f32[1,1,4,8,128]{4,0,3,2,1:T(1,128)S(1)} fusion(bf16[3,3,3,256,128]{4,3,2,1,0:T(8,128)(2,1)S(1)} %copy-done, bf16[1,3,6,8,256]{4,3,2,1,0:T(8,128)(2,1)S(1)} %fusion.37), kind=kOutput, calls=%fused_computation.35 | convolution fusion | flops 51904512 | bytes 1859584 | tf_op jit(solution)/shard_map/conv_general_dilated | solution.py:21
  53.9 0.6 %maximum_convert_fusion.2 = bf16[1,4,8,128]{3,2,1,0:T(8,128)(2,1)} fusion(f32[1,4,8,128]{3,2,1,0:T(8,128)S(1)} %bitcast.51, f32[128]{0:T(128)S(1)} %copy-done.3), kind=kLoop, calls=%fused_computation.50 | loop fusion | flops 12288 | bytes 25088 | tf_op jit(solution)/shard_map/convert_element_type | solution.py:29
  (21 shorter events, 0.3 us)
Async XLA Ops:
  0.6 52.6 %copy-start = (bf16[3,3,3,256,128]{4,3,2,1,0:T(8,128)(2,1)S(1)}, bf16[3,3,3,256,128]{4,3,2,1,0:T(8,128)(2,1)}, u32[]{:S(2)}) copy-start(bf16[3,3,3,256,128]{4,3,2,1,0:T(8,128)(2,1)} %param.12) | copy-start | bytes 5308420
  1.6 6.7 %collective-permute-start = (bf16[1,4,32,128]{3,2,1,0:T(8,128)(2,1)S(1)}, bf16[1,4,32,128]{3,2,1,0:T(8,128)(2,1)S(1)}, u32[]{:S(2)}, u32[]{:S(2)}) collective-permute-start(bf16[1,4,32,128]{3,2,1,0:T(8,128)(2,1)S(1)} %get-tuple-element.15), channel_id=1, source_target_pairs={{0,4},{4,8},{8,12},{12,16},{16,20},{20,24},{24,28},{1,5},{5,9},{9,... | collective-permute-start | bytes 98312 | tf_op jit(solution)/shard_map/ppermute | solution.py:14
  5.0 5.8 %collective-permute-start.1 = (bf16[1,4,32,128]{3,2,1,0:T(8,128)(2,1)S(1)}, bf16[1,4,32,128]{3,2,1,0:T(8,128)(2,1)S(1)}, u32[]{:S(2)}, u32[]{:S(2)}) collective-permute-start(bf16[1,4,32,128]{3,2,1,0:T(8,128)(2,1)S(1)} %get-tuple-element.14), channel_id=1, source_target_pairs={{4,0},{8,4},{12,8},{16,12},{20,16},{24,20},{28,24},{5,1},{9,5},{13... | collective-permute-start | bytes 98312 | tf_op jit(solution)/shard_map/ppermute | solution.py:15
  10.8 6.7 %copy-start.4 = (bf16[3,3,3,128,128]{4,3,2,1,0:T(8,128)(2,1)S(1)}, bf16[3,3,3,128,128]{4,3,2,1,0:T(8,128)(2,1)}, u32[]{:S(2)}) copy-start(bf16[3,3,3,128,128]{4,3,2,1,0:T(8,128)(2,1)} %param.8) | copy-start | bytes 2654212
  10.8 6.7 %copy-start.6 = (pred[8,5]{0,1:T(8,128)(4,1)S(1)}, pred[8,5]{0,1:T(8,128)(4,1)}, u32[]{:S(2)}) copy-start(pred[8,5]{0,1:T(8,128)(4,1)} %constant.22) | copy-start | bytes 124
  10.8 2.7 %collective-permute-start.2 = (bf16[6,1,32,128]{3,2,1,0:T(8,128)(2,1)S(1)}, bf16[6,1,32,128]{3,2,1,0:T(8,128)(2,1)S(1)}, u32[]{:S(2)}, u32[]{:S(2)}) collective-permute-start(bf16[6,1,32,128]{3,2,1,0:T(8,128)(2,1)S(1)} %get-tuple-element.12), channel_id=1, source_target_pairs={{0,1},{1,2},{2,3},{4,5},{5,6},{6,7},{8,9},{9,10},{10,11},{12,13},{... | collective-permute-start | bytes 147464 | tf_op jit(solution)/shard_map/ppermute | solution.py:14
  12.2 4.9 %collective-permute-start.3 = (bf16[6,1,32,128]{3,2,1,0:T(8,128)(2,1)S(1)}, bf16[6,1,32,128]{3,2,1,0:T(8,128)(2,1)S(1)}, u32[]{:S(2)}, u32[]{:S(2)}) collective-permute-start(bf16[6,1,32,128]{3,2,1,0:T(8,128)(2,1)S(1)} %get-tuple-element.13), channel_id=1, source_target_pairs={{1,0},{2,1},{3,2},{5,4},{6,5},{7,6},{9,8},{10,9},{11,10},{13,12},{... | collective-permute-start | bytes 147464 | tf_op jit(solution)/shard_map/ppermute | solution.py:15
  17.5 1.5 %copy-start.1 = (f32[128]{0:T(128)S(1)}, f32[128]{0:T(128)}, u32[]{:S(2)}) copy-start(f32[128]{0:T(128)} %param.9) | copy-start | bytes 1540
  18.9 15.6 %copy-start.2 = (f32[64]{0:T(128)S(1)}, f32[64]{0:T(128)}, u32[]{:S(2)}) copy-start(f32[64]{0:T(128)} %param.11) | copy-start | bytes 772
  19.0 15.6 %copy-start.5 = (bf16[3,3,3,128,64]{3,4,2,1,0:T(8,128)(2,1)S(1)}, bf16[3,3,3,128,64]{3,4,2,1,0:T(8,128)(2,1)}, u32[]{:S(2)}) copy-start(bf16[3,3,3,128,64]{3,4,2,1,0:T(8,128)(2,1)} %param.10) | copy-start | bytes 1327108
  19.0 15.6 %copy-start.7 = (pred[8,3]{0,1:T(4,128)(4,1)S(1)}, pred[8,3]{0,1:T(4,128)(4,1)}, u32[]{:S(2)}) copy-start(pred[8,3]{0,1:T(4,128)(4,1)} %constant.23) | copy-start | bytes 76
  25.9 7.5 %collective-permute-start.4 = (bf16[1,8,16,128]{3,2,0,1:T(8,128)(2,1)S(1)}, bf16[1,8,16,128]{3,2,0,1:T(8,128)(2,1)S(1)}, u32[]{:S(2)}, u32[]{:S(2)}) collective-permute-start(bf16[1,8,16,128]{3,2,0,1:T(8,128)(2,1)S(1)} %get-tuple-element.16), channel_id=1, source_target_pairs={{0,4},{4,8},{8,12},{12,16},{16,20},{20,24},{24,28},{1,5},{5,9},{9,... | collective-permute-start | bytes 98312 | tf_op jit(solution)/shard_map/ppermute | solution.py:14
  27.9 6.4 %collective-permute-start.5 = (bf16[1,8,16,128]{3,2,0,1:T(8,128)(2,1)S(1)}, bf16[1,8,16,128]{3,2,0,1:T(8,128)(2,1)S(1)}, u32[]{:S(2)}, u32[]{:S(2)}) collective-permute-start(bf16[1,8,16,128]{3,2,0,1:T(8,128)(2,1)S(1)} %get-tuple-element.17), channel_id=1, source_target_pairs={{4,0},{8,4},{12,8},{16,12},{20,16},{24,20},{28,24},{5,1},{9,5},{13... | collective-permute-start | bytes 98312 | tf_op jit(solution)/shard_map/ppermute | solution.py:15
  41.6 7.8 %collective-permute-start.7 = (bf16[1,4,8,256]{3,2,1,0:T(8,128)(2,1)S(1)}, bf16[1,4,8,256]{3,2,1,0:T(8,128)(2,1)S(1)}, u32[]{:S(2)}, u32[]{:S(2)}) collective-permute-start(bf16[1,4,8,256]{3,2,1,0:T(8,128)(2,1)S(1)} %bitcast.48), channel_id=1, source_target_pairs={{4,0},{8,4},{12,8},{16,12},{20,16},{24,20},{28,24},{5,1},{9,5},{13... | collective-permute-start | bytes 49160 | tf_op jit(solution)/shard_map/ppermute | solution.py:15
  46.7 6.5 %collective-permute-start.6 = (bf16[1,4,8,256]{3,2,1,0:T(8,128)(2,1)S(1)}, bf16[1,4,8,256]{3,2,1,0:T(8,128)(2,1)S(1)}, u32[]{:S(2)}, u32[]{:S(2)}) collective-permute-start(bf16[1,4,8,256]{3,2,1,0:T(8,128)(2,1)S(1)} %bitcast.49), channel_id=1, source_target_pairs={{0,4},{4,8},{8,12},{12,16},{16,20},{20,24},{24,28},{1,5},{5,9},{9,... | collective-permute-start | bytes 49160 | tf_op jit(solution)/shard_map/ppermute | solution.py:14
  48.7 5.2 %copy-start.3 = (f32[128]{0:T(128)S(1)}, f32[128]{0:T(128)}, u32[]{:S(2)}) copy-start(f32[128]{0:T(128)} %param.13) | copy-start | bytes 1540
where the time goes:
time: 54.8 us; the launch traced here: 54.5 us
  starting transfers between devices  23.2 us (42%)
  blocking collectives  12.5 us (23%)
  waiting for transfers between devices  9.79 us (18%)
  local copies, waits for them, and re-layouts  4.2 us (8%)
  matrix products  2.75 us (5%)
  other arithmetic  1.04 us (2%)
  between operations  1.02 us (2%)
    ppermute x4, starting transfers between devices, extended(): after = lax.ppermute(first, axis, down)  14.6 us
    ppermute x4, starting transfers between devices, extended(): before = lax.ppermute(last, axis, up)  8.64 us
    all_gather x1, blocking collectives, on_device(): gathered = lax.all_gather(pooled_a, 'gy', axis=1, tiled=True)  6.7 us
    ppermute x4, waiting for transfers between devices, extended(): after = lax.ppermute(first, axis, down)  5.9 us
    all_gather x1, blocking collectives, on_device(): widened = lax.all_gather(pooled_b, 'gy', axis=3, tiled=True)  5.78 us
    ppermute x4, waiting for transfers between devices, extended(): before = lax.ppermute(last, axis, up)  3.88 us
    conv_general_dilated x3, matrix products, conv_relu(): lax.conv_general_dilated(padded[None], kernel, (1, 1, 1), ((0, 0), (0, 0)...  2.75 us
    unnamed x22, local copies, waits for them, and re-layouts  2.49 us
  transfers between devices with their start and end apart: 8, of which 4 were waited for; matrix products, arithmetic and copies ran while one was open for 4% of the time, Pallas kernels for 0%

commit v1 on v0

v1 whole, which is shorter than its diff:
```python
import functools

import jax
import jax.numpy as jnp
from jax import lax
from jax.experimental import pallas as pl
from jax.experimental.pallas import tpu as pltpu
from jax.sharding import PartitionSpec as P

F32 = jnp.float32
BF16 = jnp.bfloat16
MESH = pl.DeviceIdType.MESH


def tapped(rows, width):
    count = rows.shape[0]
    x = lax.broadcasted_iota(jnp.int32, rows.shape, 0) % width
    left = jnp.where(x == 0, 0.0, pltpu.roll(rows, 1, 0))
    right = jnp.where(x == width - 1, 0.0, pltpu.roll(rows, count - 1, 0))
    return jnp.concatenate([left, rows, right], axis=-1)


def dot(a, b):
    return jnp.dot(a, b, preferred_element_type=F32)


def kernel(
    n_z, n_y,
    vol, ka, ba, kb, bb, kc, bc,
    out_a, out_b, out_c,
    loc, hz, hy, wa, wb, wc,
    sa, sz, sy, acc_a, pool_a, ga, sb, acc_b, pool_b, gb, sc,
    load_sem, hs_sem, hr_sem, as_sem, ar_sem, bs_sem, br_sem,
):
    z = lax.axis_index("gz")
    y = lax.axis_index("gy")
    d, h, xw, ca = vol.shape
    d2, h2, x2 = d // 2, h // 2, xw // 2
    hh = h2 * n_y
    cb = kb.shape[-1]
    h4, x4 = hh // 2, x2 // 2
    lanes = gb.shape[-1]
    per = lanes // cb

    loads = [
        pltpu.make_async_copy(vol, loc, load_sem.at[0]),
        pltpu.make_async_copy(ka, wa, load_sem.at[1]),
        pltpu.make_async_copy(kb, wb, load_sem.at[2]),
        pltpu.make_async_copy(kc, wc, load_sem.at[3]),
    ]
    for load in loads:
        load.start()

    has_lo, has_hi = z > 0, z < n_z - 1

    barrier = pltpu.get_barrier_semaphore()
    for away, has in ((-1, has_lo), (1, has_hi)):
        @pl.when(has)
        def _():
            for k in range(n_y):
                pl.semaphore_signal(barrier, inc=1, device_id=(z + away, k), device_id_type=MESH)
    for k in range(1, n_y):
        pl.semaphore_signal(barrier, inc=1, device_id=(z, lax.rem(y + k, n_y)), device_id_type=MESH)
    sides = jnp.where(has_lo, 1, 0) + jnp.where(has_hi, 1, 0)

    def halo(index, dz, dy):
        layer = d - 1 if dz > 0 else 0
        row = h - 1 if dy > 0 else 0
        slot = 0 if dz > 0 else 1
        if dz == 0:
            src, dst = vol.at[:, row], hy.at[0 if dy > 0 else 1]
        elif dy == 0:
            src, dst = vol.at[layer], hz.at[slot, pl.ds(1, h)]
        else:
            src, dst = vol.at[layer, row], hz.at[slot, 0 if dy > 0 else h + 1]
        return pltpu.make_async_remote_copy(
            src_ref=src, dst_ref=dst, send_sem=hs_sem.at[index], recv_sem=hr_sem.at[index],
            device_id=(z + dz, y + dy), device_id_type=MESH,
        )

    def inside(dz, dy):
        ok = None
        for pos, count, step in ((z, n_z, dz), (y, n_y, dy)):
            if step:
                one = pos > 0 if step < 0 else pos < count - 1
                ok = one if ok is None else jnp.logical_and(ok, one)
        return ok

    moves = [(-1, 0), (1, 0), (-1, -1), (-1, 1), (1, -1), (1, 1), (0, -1), (0, 1)]
    pl.semaphore_wait(barrier, sides * n_y + n_y - 1)
    for index, (dz, dy) in enumerate(moves):
        @pl.when(inside(dz, dy))
        def _():
            halo(index, dz, dy).start()

    for slot, has in ((0, has_lo), (1, has_hi)):
        @pl.when(jnp.logical_not(has))
        def _():
            hz[slot] = jnp.zeros(hz.shape[1:], BF16)
            ga[slot * (d2 + 1)] = jnp.zeros(ga.shape[1:], BF16)
            gb[slot * 2] = jnp.zeros(gb.shape[1:], BF16)
    for slot, has_y, row in ((0, y > 0, 0), (1, y < n_y - 1, h + 1)):
        @pl.when(jnp.logical_not(has_y))
        def _():
            hy[slot] = jnp.zeros(hy.shape[1:], BF16)
            for s, has in ((0, has_lo), (1, has_hi)):
                @pl.when(has)
                def _():
                    hz[s, row] = jnp.zeros(hz.shape[2:], BF16)
    for row in (0, hh + 1):
        sb[:, row] = jnp.zeros((d2 + 2,) + sb.shape[2:], BF16)
    for row in (0, h4 + 1):
        sc[:, row] = jnp.zeros((3,) + sc.shape[2:], F32)
    for slot in (0, 1):
        for end in (0, d + 1):
            sy[slot, end] = jnp.zeros(sy.shape[2:], BF16)

    loads[0].wait()
    sa[...] = tapped(loc[...].astype(F32).reshape(d * h * xw, ca), xw).astype(BF16).reshape(sa.shape)
    loads[1].wait()
    k3 = 3 * ca

    def span(tap, count):
        low, high = max(0, 1 - tap), min(count, count + 1 - tap)
        return low, high, low + tap - 1, high + tap - 1

    bias = jnp.broadcast_to(ba[...], (d * h * xw, ca)).reshape(d, h, xw, ca)
    acc_a[...] = bias + dot(sa[...].reshape(d * h * xw, k3), wa[1, 1]).reshape(d, h, xw, ca)
    for i in range(3):
        for j in range(3):
            if (i, j) == (1, 1):
                continue
            z0, z1, f0, f1 = span(i, d)
            y0, y1, g0, g1 = span(j, h)
            rows = sa[f0:f1, g0:g1].reshape(-1, k3)
            acc_a[z0:z1, y0:y1] += dot(rows, wa[i, j]).reshape(z1 - z0, y1 - y0, xw, ca)

    for index, (dz, dy) in enumerate(moves):
        if dz == 0:
            @pl.when(inside(-dz, -dy))
            def _():
                halo(index, dz, dy).wait_recv()
    for slot, row, tap in ((0, 0, 0), (1, h - 1, 2)):
        sy[slot, 1:d + 1] = tapped(hy[slot].astype(F32).reshape(d * xw, ca), xw).astype(BF16).reshape(d, xw, k3)
        total = acc_a[:, row].reshape(d * xw, ca)
        for i in range(3):
            total += dot(sy[slot, i:i + d].reshape(d * xw, k3), wa[i, tap])
        acc_a[:, row] = total.reshape(d, xw, ca)
    for index, (dz, dy) in enumerate(moves):
        if dz != 0:
            @pl.when(inside(-dz, -dy))
            def _():
                halo(index, dz, dy).wait_recv()
    for slot, layer, tap in ((0, 0, 0), (1, d - 1, 2)):
        sz[slot] = tapped(hz[slot].astype(F32).reshape((h + 2) * xw, ca), xw).astype(BF16).reshape(h + 2, xw, k3)
        total = acc_a[layer].reshape(h * xw, ca)
        for j in range(3):
            total += dot(sz[slot, j:j + h].reshape(h * xw, k3), wa[tap, j])
        acc_a[layer] = total.reshape(h, xw, ca)

    full = jnp.maximum(acc_a[...], 0.0)
    paired = jnp.max(full.reshape(d2, 2, h2, 2, xw, ca), axis=(1, 3))
    pool_a[...] = paired.reshape(d2 * h2 * xw, ca)
    half = d2 * h2 * x2
    small = jnp.maximum(pool_a[pl.ds(0, half, stride=2)], pool_a[pl.ds(1, half, stride=2)])
    mine = pl.ds(y * h2, h2)
    ga[1:d2 + 1, mine] = small.astype(BF16).reshape(d2, h2, x2, ca)

    def send_lower(buf, edge_lo, edge_hi, own_layers, top, row_slice, s_sem, r_sem):
        def to_side(slot, k):
            src = buf.at[edge_lo if slot == 0 else edge_hi, row_slice]
            dst = buf.at[top if slot == 0 else 0, row_slice]
            return pltpu.make_async_remote_copy(
                src_ref=src, dst_ref=dst, send_sem=s_sem.at[slot, k], recv_sem=r_sem.at[slot, y],
                device_id=(z + (2 * slot - 1), k), device_id_type=MESH,
            )

        def to_peer(k):
            part = buf.at[own_layers, row_slice]
            return pltpu.make_async_remote_copy(
                src_ref=part, dst_ref=part, send_sem=s_sem.at[2, k], recv_sem=r_sem.at[2, y],
                device_id=(z, lax.rem(y + k, n_y)), device_id_type=MESH,
            )

        return to_side, to_peer

    def start_all(to_side, to_peer):
        for slot, has in ((0, has_lo), (1, has_hi)):
            @pl.when(has)
            def _():
                for k in range(n_y):
                    to_side(slot, k).start()
        for k in range(1, n_y):
            to_peer(k).start()

    def await_sends(to_side, to_peer):
        for slot, has in ((0, has_lo), (1, has_hi)):
            @pl.when(has)
            def _():
                for k in range(n_y):
                    to_side(slot, k).wait_send()
        for k in range(1, n_y):
            to_peer(k).wait_send()

    def recv(dst, sem, s_sem):
        pltpu.make_async_remote_copy(
            src_ref=dst, dst_ref=dst, send_sem=s_sem, recv_sem=sem, device_id=(z, y), device_id_type=MESH
        ).wait_recv()

    side_a, peer_a = send_lower(ga, 1, d2, pl.ds(1, d2), d2 + 1, mine, as_sem, ar_sem)
    start_all(side_a, peer_a)
    out_a[...] = full.astype(BF16)

    def tapped_b(first, count):
        rows = ga[first:first + count].astype(F32).reshape(count * hh * x2, ca)
        sb[first:first + count, 1:hh + 1] = tapped(rows, x2).astype(BF16).reshape(count, hh, x2, k3)

    def part_b(first, count, i):
        rows = jnp.concatenate([sb[first:first + count, j:j + hh].reshape(count * hh * x2, k3) for j in range(3)], axis=-1)
        return dot(rows, wb[i]).reshape(count, hh, x2, cb)

    loads[2].wait()
    for k in range(1, n_y):
        q = lax.rem(y + k, n_y)
        recv(ga.at[pl.ds(1, d2), pl.ds(q * h2, h2)], ar_sem.at[2, q], as_sem.at[2, k])
    tapped_b(1, d2)
    bias = jnp.broadcast_to(bb[...], (d2 * hh * x2, cb)).reshape(d2, hh, x2, cb)
    acc_b[...] = bias + part_b(1, d2, 1)
    acc_b[1:] += part_b(1, d2 - 1, 0)
    acc_b[:d2 - 1] += part_b(2, d2 - 1, 2)
    for slot, has, first, layer, i in ((1, has_lo, 0, 0, 0), (0, has_hi, d2 + 1, d2 - 1, 2)):
        @pl.when(has)
        def _():
            for k in range(n_y):
                recv(ga.at[first, pl.ds(k * h2, h2)], ar_sem.at[slot, k], as_sem.at[slot, k])
        tapped_b(first, 1)
        acc_b[layer] += part_b(first, 1, i)[0]

    full_b = jnp.maximum(acc_b[...], 0.0)
    paired = jnp.max(full_b.reshape(hh // 2, 2, x2, cb) if d2 == 1 else jnp.max(full_b, axis=0).reshape(h4, 2, x2, cb), axis=1)
    wide = []
    for q in range(per):
        parts = [jnp.where(lax.rem(y, per) == q, paired, 0.0) if p == q else jnp.zeros_like(paired) for p in range(per)]
        wide.append(jnp.concatenate(parts, axis=-1))
    pool_b[...] = functools.reduce(jnp.add, wide).reshape(h4 * x2, lanes)
    small = jnp.maximum(pool_b[pl.ds(0, h4 * x4, stride=2)], pool_b[pl.ds(1, h4 * x4, stride=2)])
    gb[1, pl.ds(y, 1)] = small.astype(BF16)[None]
    side_b, peer_b = send_lower(gb, 1, 1, 1, 2, pl.ds(y, 1), bs_sem, br_sem)
    start_all(side_b, peer_b)
    out_b[...] = full_b.astype(BF16)

    cells = h4 * x4

    def part_c(layer):
        groups = []
        for g in range(n_y // per):
            groups.append(functools.reduce(jnp.add, [gb[layer, g * per + p].astype(F32) for p in range(per)]))
        rows = jnp.concatenate(groups, axis=-1)
        sc[layer, 1:h4 + 1] = tapped(rows, x4).reshape(h4, x4, sc.shape[-1])
        lhs = jnp.concatenate([sc[layer, j:j + h4].reshape(cells, sc.shape[-1]) for j in range(3)], axis=-1)
        return dot(lhs.astype(BF16), wc[layer])

    loads[3].wait()
    for k in range(1, n_y):
        q = lax.rem(y + k, n_y)
        recv(gb.at[1, pl.ds(q, 1)], br_sem.at[2, q], bs_sem.at[2, k])
    total = bc[...] + part_c(1)
    for slot, has, layer in ((1, has_lo, 0), (0, has_hi, 2)):
        @pl.when(has)
        def _():
            for k in range(n_y):
                recv(gb.at[layer, pl.ds(k, 1)], br_sem.at[slot, k], bs_sem.at[slot, k])
    total += part_c(0) + part_c(2)
    out_c[...] = jnp.maximum(total, 0.0).astype(BF16)

    for index, (dz, dy) in enumerate(moves):
        @pl.when(inside(dz, dy))
        def _():
            halo(index, dz, dy).wait_send()
    await_sends(side_a, peer_a)
    await_sends(side_b, peer_b)


def on_device(n_z, n_y, volume, kernel_a, bias_a, kernel_b, bias_b, kernel_c, bias_c):
    d, h, xw, ca = volume.shape
    cb, cc = kernel_b.shape[-1], kernel_c.shape[-1]
    c_in = kernel_c.shape[-2]
    d2, h2, x2 = d // 2, h // 2, xw // 2
    hh = h2 * n_y
    h4, x4 = hh // 2, x2 // 2
    lanes = 128
    wa = kernel_a.reshape(3, 3, 3 * ca, ca)
    wb = kernel_b.reshape(3, 9 * ca, cb)
    wc = kernel_c.reshape(3, 9 * c_in, cc)
    vmem = pl.BlockSpec(memory_space=pltpu.VMEM)
    hbm = pl.BlockSpec(memory_space=pl.ANY)
    out_a, out_b, out_c = pl.pallas_call(
        functools.partial(kernel, n_z, n_y),
        out_shape=(
            jax.ShapeDtypeStruct((d, h, xw, ca), BF16),
            jax.ShapeDtypeStruct((d2, hh, x2, cb), BF16),
            jax.ShapeDtypeStruct((h4 * x4, cc), BF16),
        ),
        in_specs=[hbm, hbm, vmem, hbm, vmem, hbm, vmem],
        out_specs=(vmem, vmem, vmem),
        scratch_shapes=[
            pltpu.VMEM(volume.shape, BF16),
            pltpu.VMEM((2, h + 2, xw, ca), BF16),
            pltpu.VMEM((2, d, xw, ca), BF16),
            pltpu.VMEM(wa.shape, BF16),
            pltpu.VMEM(wb.shape, BF16),
            pltpu.VMEM(wc.shape, BF16),
            pltpu.VMEM((d, h, xw, 3 * ca), BF16),
            pltpu.VMEM((2, h + 2, xw, 3 * ca), BF16),
            pltpu.VMEM((2, d + 2, xw, 3 * ca), BF16),
            pltpu.VMEM((d, h, xw, ca), F32),
            pltpu.VMEM((d2 * h2 * xw, ca), F32),
            pltpu.VMEM((d2 + 2, hh, x2, ca), BF16),
            pltpu.VMEM((d2 + 2, hh + 2, x2, 3 * ca), BF16),
            pltpu.VMEM((d2, hh, x2, cb), F32),
            pltpu.VMEM((h4 * x2, lanes), F32),
            pltpu.VMEM((3, n_y, h4 * x4, lanes), BF16),
            pltpu.VMEM((3, h4 + 2, x4, 3 * c_in), F32),
            pltpu.SemaphoreType.DMA((4,)),
            pltpu.SemaphoreType.DMA((8,)),
            pltpu.SemaphoreType.DMA((8,)),
            pltpu.SemaphoreType.DMA((3, n_y)),
            pltpu.SemaphoreType.DMA((3, n_y)),
            pltpu.SemaphoreType.DMA((3, n_y)),
            pltpu.SemaphoreType.DMA((3, n_y)),
        ],
        compiler_params=pltpu.CompilerParams(collective_id=0, has_side_effects=True),
        name="unet",
    )(volume, wa, bias_a.reshape(1, -1), wb, bias_b.reshape(1, -1), wc, bias_c.reshape(1, -1))
    return out_a, out_b, out_c.reshape(d2 // 2, h4, x4, cc)


def solution(mesh):
    sizes = dict(mesh.shape)
    return jax.shard_map(
        functools.partial(on_device, sizes["gz"], sizes["gy"]),
        mesh=mesh,
        in_specs=(
            P("gz", "gy", None, None),
            P(),
            P(),
            P(None, None, None, None, "gy"),
            P("gy"),
            P(None, None, None, None, "gy"),
            P("gy"),
        ),
        out_specs=(P("gz", "gy", None, None), P("gz", None, None, "gy"), P("gz", None, None, "gy")),
        check_vma=False,
    )
```

time: 54.8 us -> 26.3 us (0.48)
  the two profiles are of different devices: /device:TPU:24 before, /device:TPU:0 now
where the time goes in v1:
time: 26.3 us; the launch traced here: 26 us
  Pallas kernels  18.8 us (71%)
  local copies, waits for them, and re-layouts  6.58 us (25%)
  between operations  0.64 us (2%)
    pallas_call x1, Pallas kernels, on_device(): pl.pallas_call(functools.partial(kernel, n_z, n_y), out_shape=(jax.ShapeD...  18.8 us
    unnamed x4, local copies, waits for them, and re-layouts  6.58 us

profile of v1, /device:TPU:0, one launch (start us, length us, event | category | flops | bytes accessed | tf_op | source)
XLA Modules:
  0.0 26.0 jit_solution(1331968559697693662)
XLA Ops:
  0.6 2.2 %copy.10 = bf16[3,3,3,128,64]{4,3,2,1,0:T(8,128)(2,1)} copy(bf16[3,3,3,128,64]{3,4,2,1,0:T(8,128)(2,1)} %param.10) | data formatting | bytes 884736 | tf_op args[3]
  2.9 18.8 %unet.1 = (bf16[4,4,32,128]{3,2,1,0:T(8,128)(2,1)}, bf16[2,8,16,64]{3,2,1,0:T(8,128)(2,1)}, bf16[32,128]{1,0:T(8,128)(2,1)}) custom-call(bf16[4,4,32,128]{3,2,1,0:T(8,128)(2,1)} %vol.1, bf16[3,3,384,128]{3,2,1,0:T(8,128)(2,1)} %bitcast.9, f32[1,128]{1,0:T(1,128)} %bitcast.11, bf16[3,1152,64]{2,1,0:T(8,128)(2,1)} %bitcast.7, f32[1,64]{1,0:T(1,128)} %bitcast.12, ...), custom_call_target="tpu_custom_call" | custom-call | tf_op jit(solution)/shard_map/unet/pallas_call | solution.py:297
  21.7 1.6 %copy.14 = bf16[4,4,32,128]{3,2,1,0:T(8,128)(2,1)} copy(bf16[4,4,32,128]{3,2,1,0:T(8,128)(2,1)} %get-tuple-element.12) | data formatting | bytes 262144
  23.2 1.5 %copy.15 = bf16[2,8,16,64]{3,2,1,0:T(8,128)(2,1)} copy(bf16[2,8,16,64]{3,2,1,0:T(8,128)(2,1)} %get-tuple-element.13) | data formatting | bytes 65536
  24.7 1.3 %copy.16 = bf16[1,4,8,128]{3,2,1,0:T(8,128)(2,1)} copy(bf16[1,4,8,128]{3,2,1,0:T(8,128)(2,1)} %bitcast.10) | data formatting | bytes 16384

commit v2 on v1

--- a/solution.py
+++ b/solution.py
@@ -28,7 +28,7 @@
     n_z, n_y,
     vol, ka, ba, kb, bb, kc, bc,
     out_a, out_b, out_c,
-    loc, hz, hy, wa, wb, wc,
+    loc, hz, hy, wa, wt, wb, wc,
     sa, sz, sy, acc_a, pool_a, ga, sb, acc_b, pool_b, gb, sc,
     load_sem, hs_sem, hr_sem, as_sem, ar_sem, bs_sem, br_sem,
 ):
@@ -37,7 +37,7 @@
     d, h, xw, ca = vol.shape
     d2, h2, x2 = d // 2, h // 2, xw // 2
     hh = h2 * n_y
-    cb = kb.shape[-1]
+    cb = kb.shape[-2]
     h4, x4 = hh // 2, x2 // 2
     lanes = gb.shape[-1]
     per = lanes // cb
@@ -45,7 +45,7 @@
     loads = [
         pltpu.make_async_copy(vol, loc, load_sem.at[0]),
         pltpu.make_async_copy(ka, wa, load_sem.at[1]),
-        pltpu.make_async_copy(kb, wb, load_sem.at[2]),
+        pltpu.make_async_copy(kb, wt, load_sem.at[2]),
         pltpu.make_async_copy(kc, wc, load_sem.at[3]),
     ]
     for load in loads:
@@ -220,6 +220,9 @@
         return dot(rows, wb[i]).reshape(count, hh, x2, cb)
 
     loads[2].wait()
+    for i in range(3):
+        for tap in range(9):
+            wb[i, tap * ca:(tap + 1) * ca] = wt[9 * i + tap].T
     for k in range(1, n_y):
         q = lax.rem(y + k, n_y)
         recv(ga.at[pl.ds(1, d2), pl.ds(q * h2, h2)], ar_sem.at[2, q], as_sem.at[2, k])
@@ -281,6 +284,15 @@
     await_sends(side_b, peer_b)
 
 
+def put_out(*refs):
+    sem = refs[-1]
+    copies = [pltpu.make_async_copy(refs[i], refs[i + 3], sem.at[i]) for i in range(3)]
+    for copy in copies:
+        copy.start()
+    for copy in copies:
+        copy.wait()
+
+
 def on_device(n_z, n_y, volume, kernel_a, bias_a, kernel_b, bias_b, kernel_c, bias_c):
     d, h, xw, ca = volume.shape
     cb, cc = kernel_b.shape[-1], kernel_c.shape[-1]
@@ -290,17 +302,14 @@
     h4, x4 = hh // 2, x2 // 2
     lanes = 128
     wa = kernel_a.reshape(3, 3, 3 * ca, ca)
-    wb = kernel_b.reshape(3, 9 * ca, cb)
+    wb = jnp.swapaxes(kernel_b, 3, 4).reshape(27, cb, ca)
     wc = kernel_c.reshape(3, 9 * c_in, cc)
     vmem = pl.BlockSpec(memory_space=pltpu.VMEM)
     hbm = pl.BlockSpec(memory_space=pl.ANY)
-    out_a, out_b, out_c = pl.pallas_call(
+    shapes = ((d, h, xw, ca), (d2, hh, x2, cb), (h4 * x4, cc))
+    results = pl.pallas_call(
         functools.partial(kernel, n_z, n_y),
-        out_shape=(
-            jax.ShapeDtypeStruct((d, h, xw, ca), BF16),
-            jax.ShapeDtypeStruct((d2, hh, x2, cb), BF16),
-            jax.ShapeDtypeStruct((h4 * x4, cc), BF16),
-        ),
+        out_shape=tuple(pltpu.VMEM(shape, BF16) for shape in shapes),
         in_specs=[hbm, hbm, vmem, hbm, vmem, hbm, vmem],
         out_specs=(vmem, vmem, vmem),
         scratch_shapes=[
@@ -309,6 +318,7 @@
             pltpu.VMEM((2, d, xw, ca), BF16),
             pltpu.VMEM(wa.shape, BF16),
             pltpu.VMEM(wb.shape, BF16),
+            pltpu.VMEM((3, 9 * ca, cb), BF16),
             pltpu.VMEM(wc.shape, BF16),
             pltpu.VMEM((d, h, xw, 3 * ca), BF16),
             pltpu.VMEM((2, h + 2, xw, 3 * ca), BF16),
@@ -332,6 +342,14 @@
         compiler_params=pltpu.CompilerParams(collective_id=0, has_side_effects=True),
         name="unet",
     )(volume, wa, bias_a.reshape(1, -1), wb, bias_b.reshape(1, -1), wc, bias_c.reshape(1, -1))
+    out_a, out_b, out_c = pl.pallas_call(
+        put_out,
+        out_shape=tuple(jax.ShapeDtypeStruct(shape, BF16) for shape in shapes),
+        in_specs=[vmem] * 3,
+        out_specs=(hbm,) * 3,
+        scratch_shapes=[pltpu.SemaphoreType.DMA((3,))],
+        name="put_out",
+    )(*[pltpu.with_memory_space_constraint(r, pltpu.VMEM) for r in results])
     return out_a, out_b, out_c.reshape(d2 // 2, h4, x4, cc)
 
 

time: 26.3 us -> 19.6 us (0.75)
  local copies, waits for them, and re-layouts: 6.58 us -> 0 us
    unnamed x4 -> x0, local copies, waits for them, and re-layouts: 6.58 us -> none
    pallas_call x1 -> x2, Pallas kernels: 18.8 us -> 18.8 us  [the longest x1 18.1 us: on_device(): pl.pallas_call(functools.partial(kernel, n_z, n_y), out_shape=tuple((pltp...]
where the time goes in v2:
time: 19.6 us; the launch traced here: 19.5 us
  Pallas kernels  18.8 us (96%)
  between operations  0.64 us (3%)
    pallas_call x1, Pallas kernels, on_device(): pl.pallas_call(functools.partial(kernel, n_z, n_y), out_shape=tuple((pltp...  18.1 us
    pallas_call x1, Pallas kernels, on_device(): pl.pallas_call(put_out, out_shape=tuple((jax.ShapeDtypeStruct(shape, BF16...  0.7 us

profile of v2, /device:TPU:0, one launch (start us, length us, event | category | flops | bytes accessed | tf_op | source)
XLA Modules:
  0.0 19.5 jit_solution(11837339830097866111)
XLA Ops:
  0.6 18.1 %unet.1 = (bf16[4,4,32,128]{3,2,1,0:T(8,128)(2,1)S(1)}, bf16[2,8,16,64]{3,2,1,0:T(8,128)(2,1)S(1)}, bf16[32,128]{1,0:T(8,128)(2,1)S(1)}) custom-call(bf16[4,4,32,128]{3,2,1,0:T(8,128)(2,1)} %vol.1, bf16[3,3,384,128]{3,2,1,0:T(8,128)(2,1)} %bitcast.10, f32[1,128]{1,0:T(1,128)} %bitcast.12, bf16[27,64,128]{2,1,0:T(8,128)(2,1)} %bitcast.11, f32[1,64]{1,0:T(1,128)} %bitcast.13, ...), custom_call_target="tpu_custom_call" | custom-call | tf_op jit(solution)/shard_map/unet/pallas_call | solution.py:310
  18.8 0.7 %put_out.1 = (bf16[4,4,32,128]{3,2,1,0:T(8,128)(2,1)}, bf16[2,8,16,64]{3,2,1,0:T(8,128)(2,1)}, bf16[32,128]{1,0:T(8,128)(2,1)}) custom-call(bf16[4,4,32,128]{3,2,1,0:T(8,128)(2,1)S(1)} %get-tuple-element.9.refs_0_, bf16[2,8,16,64]{3,2,1,0:T(8,128)(2,1)S(1)} %get-tuple-element.10.refs_1_, bf16[32,128]{1,0:T(8,128)(2,1)S(1)} %get-tuple-element.11.refs_2_), custom_call_target="tpu_custom_call" | custom-call | tf_op jit(solution)/shard_map/put_out/pallas_call | solution.py:345

commit v3 on v2

--- a/solution.py
+++ b/solution.py
@@ -26,11 +26,11 @@
 
 def kernel(
     n_z, n_y,
-    vol, ka, ba, kb, bb, kc, bc,
+    vol, ka, bias_a, kb, bias_b, kc, bias_c,
     out_a, out_b, out_c,
-    loc, hz, hy, wa, wt, wb, wc,
+    loc, hz, hy, wa, wt, wb, wc, ba, bb, bc,
     sa, sz, sy, acc_a, pool_a, ga, sb, acc_b, pool_b, gb, sc,
-    load_sem, hs_sem, hr_sem, as_sem, ar_sem, bs_sem, br_sem,
+    perm, load_sem, hs_sem, hr_sem, as_sem, ar_sem, bs_sem, br_sem,
 ):
     z = lax.axis_index("gz")
     y = lax.axis_index("gy")
@@ -47,9 +47,10 @@
         pltpu.make_async_copy(ka, wa, load_sem.at[1]),
         pltpu.make_async_copy(kb, wt, load_sem.at[2]),
         pltpu.make_async_copy(kc, wc, load_sem.at[3]),
+        pltpu.make_async_copy(bias_a, ba, load_sem.at[4]),
+        pltpu.make_async_copy(bias_b, bb, load_sem.at[5]),
+        pltpu.make_async_copy(bias_c, bc, load_sem.at[6]),
     ]
-    for load in loads:
-        load.start()
 
     has_lo, has_hi = z > 0, z < n_z - 1
 
@@ -57,10 +58,11 @@
     for away, has in ((-1, has_lo), (1, has_hi)):
         @pl.when(has)
         def _():
-            for k in range(n_y):
-                pl.semaphore_signal(barrier, inc=1, device_id=(z + away, k), device_id_type=MESH)
+            pl.semaphore_signal(barrier, inc=1, device_id=(z + away, y), device_id_type=MESH)
     for k in range(1, n_y):
         pl.semaphore_signal(barrier, inc=1, device_id=(z, lax.rem(y + k, n_y)), device_id_type=MESH)
+    for load in loads:
+        load.start()
     sides = jnp.where(has_lo, 1, 0) + jnp.where(has_hi, 1, 0)
 
     def halo(index, dz, dy):
@@ -87,11 +89,25 @@
         return ok
 
     moves = [(-1, 0), (1, 0), (-1, -1), (-1, 1), (1, -1), (1, 1), (0, -1), (0, 1)]
-    pl.semaphore_wait(barrier, sides * n_y + n_y - 1)
+    pl.semaphore_wait(barrier, sides + n_y - 1)
+    for slot, dy in ((0, 1), (1, -1)):
+        @pl.when(inside(0, dy))
+        def _():
+            pl.semaphore_signal(perm.at[slot], inc=1, device_id=(z, y + dy), device_id_type=MESH)
     for index, (dz, dy) in enumerate(moves):
-        @pl.when(inside(dz, dy))
-        def _():
-            halo(index, dz, dy).start()
+        if dz == 0 or dy == 0:
+            @pl.when(inside(dz, dy))
+            def _():
+                halo(index, dz, dy).start()
+    for slot, side in ((0, -1), (1, 1)):
+        @pl.when(inside(0, side))
+        def _():
+            pl.semaphore_wait(perm.at[slot], 1)
+            for index, (dz, dy) in enumerate(moves):
+                if dz != 0 and dy == side:
+                    @pl.when(inside(dz, 0))
+                    def _():
+                        halo(index, dz, dy).start()
 
     for slot, has in ((0, has_lo), (1, has_hi)):
         @pl.when(jnp.logical_not(has))
@@ -118,6 +134,7 @@
     loads[0].wait()
     sa[...] = tapped(loc[...].astype(F32).reshape(d * h * xw, ca), xw).astype(BF16).reshape(sa.shape)
     loads[1].wait()
+    loads[4].wait()
     k3 = 3 * ca
 
     def span(tap, count):
@@ -220,6 +237,7 @@
         return dot(rows, wb[i]).reshape(count, hh, x2, cb)
 
     loads[2].wait()
+    loads[5].wait()
     for i in range(3):
         for tap in range(9):
             wb[i, tap * ca:(tap + 1) * ca] = wt[9 * i + tap].T
@@ -264,6 +282,7 @@
         return dot(lhs.astype(BF16), wc[layer])
 
     loads[3].wait()
+    loads[6].wait()
     for k in range(1, n_y):
         q = lax.rem(y + k, n_y)
         recv(gb.at[1, pl.ds(q, 1)], br_sem.at[2, q], bs_sem.at[2, k])
@@ -310,7 +329,7 @@
     results = pl.pallas_call(
         functools.partial(kernel, n_z, n_y),
         out_shape=tuple(pltpu.VMEM(shape, BF16) for shape in shapes),
-        in_specs=[hbm, hbm, vmem, hbm, vmem, hbm, vmem],
+        in_specs=[hbm] * 7,
         out_specs=(vmem, vmem, vmem),
         scratch_shapes=[
             pltpu.VMEM(volume.shape, BF16),
@@ -320,6 +339,9 @@
             pltpu.VMEM(wb.shape, BF16),
             pltpu.VMEM((3, 9 * ca, cb), BF16),
             pltpu.VMEM(wc.shape, BF16),
+            pltpu.VMEM((1, ca), F32),
+            pltpu.VMEM((1, cb), F32),
+            pltpu.VMEM((1, cc), F32),
             pltpu.VMEM((d, h, xw, 3 * ca), BF16),
             pltpu.VMEM((2, h + 2, xw, 3 * ca), BF16),
             pltpu.VMEM((2, d + 2, xw, 3 * ca), BF16),
@@ -331,7 +353,8 @@
             pltpu.VMEM((h4 * x2, lanes), F32),
             pltpu.VMEM((3, n_y, h4 * x4, lanes), BF16),
             pltpu.VMEM((3, h4 + 2, x4, 3 * c_in), F32),
-            pltpu.SemaphoreType.DMA((4,)),
+            pltpu.SemaphoreType.REGULAR((2,)),
+            pltpu.SemaphoreType.DMA((7,)),
             pltpu.SemaphoreType.DMA((8,)),
             pltpu.SemaphoreType.DMA((8,)),
             pltpu.SemaphoreType.DMA((3, n_y)),

time: 19.6 us -> 18.1 us (0.923)
  Pallas kernels: 18.8 us -> 17.3 us
    pallas_call x1, Pallas kernels: 18.1 us -> 16.6 us  [on_device(): pl.pallas_call(functools.partial(kernel, n_z, n_y), out_shape=tuple((pltp...]
where the time goes in v3:
time: 18.1 us; the launch traced here: 18 us
  Pallas kernels  17.3 us (96%)
  between operations  0.64 us (4%)
    pallas_call x1, Pallas kernels, on_device(): pl.pallas_call(functools.partial(kernel, n_z, n_y), out_shape=tuple((pltp...  16.6 us
    pallas_call x1, Pallas kernels, on_device(): pl.pallas_call(put_out, out_shape=tuple((jax.ShapeDtypeStruct(shape, BF16...  0.7 us

profile of v3, /device:TPU:0, one launch (start us, length us, event | category | flops | bytes accessed | tf_op | source)
XLA Modules:
  0.0 18.0 jit_solution(11418489352799819678)
XLA Ops:
  0.6 16.6 %unet.1 = (bf16[4,4,32,128]{3,2,1,0:T(8,128)(2,1)S(1)}, bf16[2,8,16,64]{3,2,1,0:T(8,128)(2,1)S(1)}, bf16[32,128]{1,0:T(8,128)(2,1)S(1)}) custom-call(bf16[4,4,32,128]{3,2,1,0:T(8,128)(2,1)} %vol.1, bf16[3,3,384,128]{3,2,1,0:T(8,128)(2,1)} %bitcast.10, f32[1,128]{1,0:T(1,128)} %bitcast.12, bf16[27,64,128]{2,1,0:T(8,128)(2,1)} %bitcast.11, f32[1,64]{1,0:T(1,128)} %bitcast.13, ...), custom_call_target="tpu_custom_call" | custom-call | tf_op jit(solution)/shard_map/unet/pallas_call | solution.py:329
  17.3 0.7 %put_out.1 = (bf16[4,4,32,128]{3,2,1,0:T(8,128)(2,1)}, bf16[2,8,16,64]{3,2,1,0:T(8,128)(2,1)}, bf16[32,128]{1,0:T(8,128)(2,1)}) custom-call(bf16[4,4,32,128]{3,2,1,0:T(8,128)(2,1)S(1)} %get-tuple-element.9.refs_0_, bf16[2,8,16,64]{3,2,1,0:T(8,128)(2,1)S(1)} %get-tuple-element.10.refs_1_, bf16[32,128]{1,0:T(8,128)(2,1)S(1)} %get-tuple-element.11.refs_2_), custom_call_target="tpu_custom_call" | custom-call | tf_op jit(solution)/shard_map/put_out/pallas_call | solution.py:368

commit v4 on v3

--- a/solution.py
+++ b/solution.py
@@ -163,25 +163,7 @@
         for i in range(3):
             total += dot(sy[slot, i:i + d].reshape(d * xw, k3), wa[i, tap])
         acc_a[:, row] = total.reshape(d, xw, ca)
-    for index, (dz, dy) in enumerate(moves):
-        if dz != 0:
-            @pl.when(inside(-dz, -dy))
-            def _():
-                halo(index, dz, dy).wait_recv()
-    for slot, layer, tap in ((0, 0, 0), (1, d - 1, 2)):
-        sz[slot] = tapped(hz[slot].astype(F32).reshape((h + 2) * xw, ca), xw).astype(BF16).reshape(h + 2, xw, k3)
-        total = acc_a[layer].reshape(h * xw, ca)
-        for j in range(3):
-            total += dot(sz[slot, j:j + h].reshape(h * xw, k3), wa[tap, j])
-        acc_a[layer] = total.reshape(h, xw, ca)
-
-    full = jnp.maximum(acc_a[...], 0.0)
-    paired = jnp.max(full.reshape(d2, 2, h2, 2, xw, ca), axis=(1, 3))
-    pool_a[...] = paired.reshape(d2 * h2 * xw, ca)
-    half = d2 * h2 * x2
-    small = jnp.maximum(pool_a[pl.ds(0, half, stride=2)], pool_a[pl.ds(1, half, stride=2)])
     mine = pl.ds(y * h2, h2)
-    ga[1:d2 + 1, mine] = small.astype(BF16).reshape(d2, h2, x2, ca)
 
     def send_lower(buf, edge_lo, edge_hi, own_layers, top, row_slice, s_sem, r_sem):
         def to_side(slot, k):
@@ -225,8 +207,34 @@
         ).wait_recv()
 
     side_a, peer_a = send_lower(ga, 1, d2, pl.ds(1, d2), d2 + 1, mine, as_sem, ar_sem)
-    start_all(side_a, peer_a)
-    out_a[...] = full.astype(BF16)
+
+    def pool_layer(p):
+        pair = jnp.maximum(acc_a[2 * p:2 * p + 2], 0.0)
+        pool_a[pl.ds(p * h2 * xw, h2 * xw)] = jnp.max(pair.reshape(2, h2, 2, xw, ca), axis=(0, 2)).reshape(h2 * xw, ca)
+        even, odd = (pool_a[pl.ds(p * h2 * xw + q, h2 * x2, stride=2)] for q in (0, 1))
+        ga[1 + p, mine] = jnp.maximum(even, odd).astype(BF16).reshape(h2, x2, ca)
+
+    for p in range(1, d2 - 1):
+        pool_layer(p)
+    for slot, layer, tap, has in ((0, 0, 0, has_lo), (1, d - 1, 2, has_hi)):
+        for index, (dz, dy) in enumerate(moves):
+            if dz == 1 - 2 * slot:
+                @pl.when(inside(-dz, -dy))
+                def _():
+                    halo(index, dz, dy).wait_recv()
+        sz[slot] = tapped(hz[slot].astype(F32).reshape((h + 2) * xw, ca), xw).astype(BF16).reshape(h + 2, xw, k3)
+        total = acc_a[layer].reshape(h * xw, ca)
+        for j in range(3):
+            total += dot(sz[slot, j:j + h].reshape(h * xw, k3), wa[tap, j])
+        acc_a[layer] = total.reshape(h, xw, ca)
+        pool_layer(slot * (d2 - 1))
+        @pl.when(has)
+        def _():
+            for k in range(n_y):
+                side_a(slot, k).start()
+    for k in range(1, n_y):
+        peer_a(k).start()
+    out_a[...] = jnp.maximum(acc_a[...], 0.0).astype(BF16)
 
     def tapped_b(first, count):
         rows = ga[first:first + count].astype(F32).reshape(count * hh * x2, ca)

time: 18.1 us -> 17.7 us (0.978)
  Pallas kernels: 17.3 us -> 17 us
    pallas_call x1, Pallas kernels: 16.6 us -> 16.2 us  [on_device(): pl.pallas_call(functools.partial(kernel, n_z, n_y), out_shape=tuple((pltp...]
where the time goes in v4:
time: 17.7 us; the launch traced here: 17.6 us
  Pallas kernels  17 us (96%)
  between operations  0.64 us (4%)
    pallas_call x1, Pallas kernels, on_device(): pl.pallas_call(functools.partial(kernel, n_z, n_y), out_shape=tuple((pltp...  16.2 us
    pallas_call x1, Pallas kernels, on_device(): pl.pallas_call(put_out, out_shape=tuple((jax.ShapeDtypeStruct(shape, BF16...  0.7 us

profile of v4, /device:TPU:0, one launch (start us, length us, event | category | flops | bytes accessed | tf_op | source)
XLA Modules:
  0.0 17.6 jit_solution(10604746060891783918)
XLA Ops:
  0.6 16.2 %unet.1 = (bf16[4,4,32,128]{3,2,1,0:T(8,128)(2,1)S(1)}, bf16[2,8,16,64]{3,2,1,0:T(8,128)(2,1)S(1)}, bf16[32,128]{1,0:T(8,128)(2,1)S(1)}) custom-call(bf16[4,4,32,128]{3,2,1,0:T(8,128)(2,1)} %vol.1, bf16[3,3,384,128]{3,2,1,0:T(8,128)(2,1)} %bitcast.10, f32[1,128]{1,0:T(1,128)} %bitcast.12, bf16[27,64,128]{2,1,0:T(8,128)(2,1)} %bitcast.11, f32[1,64]{1,0:T(1,128)} %bitcast.13, ...), custom_call_target="tpu_custom_call" | custom-call | tf_op jit(solution)/shard_map/unet/pallas_call | solution.py:337
  16.9 0.7 %put_out.1 = (bf16[4,4,32,128]{3,2,1,0:T(8,128)(2,1)}, bf16[2,8,16,64]{3,2,1,0:T(8,128)(2,1)}, bf16[32,128]{1,0:T(8,128)(2,1)}) custom-call(bf16[4,4,32,128]{3,2,1,0:T(8,128)(2,1)S(1)} %get-tuple-element.9.refs_0_, bf16[2,8,16,64]{3,2,1,0:T(8,128)(2,1)S(1)} %get-tuple-element.10.refs_1_, bf16[32,128]{1,0:T(8,128)(2,1)S(1)} %get-tuple-element.11.refs_2_), custom_call_target="tpu_custom_call" | custom-call | tf_op jit(solution)/shard_map/put_out/pallas_call | solution.py:376
